TPU v7x, 128 devices: a whole 4x4x4 slice. The times are simulated.
128 devices in a mesh: blk: 16 (over z, y_lo, core), exp: 8 (over y_hi, x).
Axes of the slice: x: 4, y: 4 (y_hi: 2, y_lo: 2; y = y_hi * 2 + y_lo), z: 4, core: 2. Of those that a mesh axis runs over, the one named last changes fastest.
Arguments:
- nodes: bfloat16 [24576, 512], P('blk'), may hold values from -8 to 8
- attention_weights: bfloat16 [3, 256, 512], P(None, 'exp'), may hold values from -1.5 to 1.5
- output_weight: bfloat16 [256, 512], P('exp'), may hold values from -2 to 2
- router_weight: bfloat16 [8, 512], replicated, may hold values from -1.25 to 1.25
- gain_first: float32 [512], replicated, may hold values from 0.1 to 1.9
- gain_second: float32 [512], replicated, may hold values from 0.1 to 1.9
- expert_in: bfloat16 [8, 2048, 512], P('exp', 'blk'), may hold values from -0.25 to 0.25
- expert_out: bfloat16 [8, 2048, 512], P('exp', 'blk'), may hold values from -0.125 to 0.125
- routes: int32 [24576, 2], P(('blk', 'exp')), may hold values from 0 to 7, all different within a row; in each aligned block of 192 rows (0 to 191, 192 to 383, ...) at most 96 rows name the same one
- cotangent: bfloat16 [24576, 512], P(('blk', 'exp')), may hold values from -6 to 6
Outputs:
- layer_out: bfloat16 [24576, 512], P(('blk', 'exp'))
- stream_grad: bfloat16 [24576, 512], P(('blk', 'exp'))
- expert_in_grad: float32 [8, 2048, 512], P('exp', 'blk')
- expert_out_grad: float32 [8, 2048, 512], P('exp', 'blk')
- router_grad: float32 [8, 512], replicated
- gain_grad: float32 [512], replicated
Inputs may be any that keep to these rules, and one draw needn't show every extreme that they name: `routes`: each row names two different experts. Among the rows of one device (aligned blocks of 192 rows) no expert is named by more than 96 rows, and in some block one expert is named by exactly 96 rows.
All inputs are finite; a program needn't handle non-finite values.
Results may differ from a plain program's by a relative error of at most 0.04.
The roundings to bfloat16 on the way count: a program that leaves them out, or rounds other values in their place, can miss the bound.
Values may be sent and summed in bfloat16 or wider, within the bound.
No kernel may reach another device: no remote copies, remote signals or barrier semaphores. Data moves between devices by JAX's collectives and lax.ppermute only.
A program may use at most 64 MiB of HBM per device.

v0:
```python
import math
import jax
import jax.numpy as jnp
from jax import lax
from jax.sharding import PartitionSpec as P

HD = 32
EPSILON = 1e-06
NEG_LARGE = -1e30


def rms_gain(stream, gain):
    return stream * lax.rsqrt(jnp.mean(stream * stream, axis=-1, keepdims=True) + EPSILON) * gain


def gelu_tanh(values):
    return jax.nn.gelu(values, approximate=True)


def to_sources(buffer):
    return lax.all_to_all(buffer, "exp", split_axis=0, concat_axis=0, tiled=True)


def local(
    nodes,
    attention_weights,
    output_weight,
    router_weight,
    gain_first,
    gain_second,
    expert_in,
    expert_out,
    routes,
    cotangent,
):
    exp_count = lax.axis_size("exp")
    blk_count = lax.axis_size("blk")
    block_rows = nodes.shape[0]
    width = nodes.shape[1]
    features = attention_weights.shape[1]
    heads_here = features // HD
    own_rows = block_rows // exp_count
    capacity = 4 * block_rows // (exp_count * exp_count)
    experts = router_weight.shape[0]
    grad_scale = 1.0 / math.sqrt(block_rows * blk_count)
    score_scale = 1.0 / math.sqrt(HD)
    query = jnp.einsum(
        "td,fd->tf", nodes, attention_weights[0], preferred_element_type=jnp.float32
    ).astype(jnp.bfloat16)
    query_heads = query.reshape(block_rows, heads_here, HD).transpose(1, 0, 2)
    keys_values = jnp.einsum(
        "td,cfd->cft", nodes, attention_weights[1:], preferred_element_type=jnp.float32
    ).astype(jnp.bfloat16)
    start_state = (
        jnp.full((heads_here, block_rows), NEG_LARGE, jnp.float32),
        jnp.zeros((heads_here, block_rows), jnp.float32),
        jnp.zeros((heads_here, block_rows, HD), jnp.float32),
    )
    totals = start_state
    shard_piece = lax.all_gather(keys_values, "blk", axis=2, tiled=True)
    length = shard_piece.shape[2]
    key_width = math.gcd(length, 1024)
    key_blocks = shard_piece.reshape(2, heads_here, HD, length // key_width, key_width).transpose(
        3, 0, 1, 2, 4
    )

    def key_step(running, key_block):
        run_max, run_sum, accum = running
        scores = (
            jnp.einsum(
                "htf,hfk->htk", query_heads, key_block[0], preferred_element_type=jnp.float32
            )
            * score_scale
        )
        new_max = jnp.maximum(run_max, jnp.max(scores, axis=-1))
        shrink = jnp.exp(run_max - new_max)
        weights = jnp.exp(scores - new_max[..., None])
        run_sum = run_sum * shrink + jnp.sum(weights, axis=-1)
        update = jnp.einsum(
            "htk,hfk->htf",
            weights.astype(jnp.bfloat16),
            key_block[1],
            preferred_element_type=jnp.float32,
        )
        accum = accum * shrink[..., None] + update
        return ((new_max, run_sum, accum), None)

    totals, _ = lax.scan(key_step, totals, key_blocks)
    run_max, run_sum, accum = totals
    attended = (accum / run_sum[..., None]).astype(jnp.bfloat16)
    by_rows = attended.transpose(1, 0, 2).reshape(block_rows, features)
    attn_out = lax.psum_scatter(
        jnp.dot(by_rows, output_weight, preferred_element_type=jnp.float32).astype(jnp.bfloat16),
        "exp",
        scatter_dimension=0,
        tiled=True,
    ).astype(jnp.float32)
    own_nodes = lax.dynamic_slice_in_dim(
        nodes, lax.axis_index("exp") * own_rows, own_rows, 0
    ).astype(jnp.float32)
    stream = rms_gain(own_nodes + attn_out, gain_first).astype(jnp.bfloat16)
    logits = jnp.dot(stream, router_weight.T, preferred_element_type=jnp.float32)
    flat_routes = routes.reshape(2 * own_rows)
    choose = (flat_routes[:, None] == jnp.arange(experts, dtype=jnp.int32)[None, :]).astype(
        jnp.int32
    )
    before = jnp.cumsum(choose, axis=0) - choose
    slot_index = jnp.sum(before * choose, axis=1)
    position = flat_routes * capacity + slot_index
    dispatch_table = (
        jnp.arange(experts * capacity, dtype=jnp.int32)[:, None] == position[None, :]
    ).astype(jnp.bfloat16)
    selected = choose.reshape(own_rows, 2, experts).astype(jnp.float32)

    def gate_values(values):
        picked = jnp.sum(jax.nn.sigmoid(values)[:, None, :] * selected, axis=-1)
        return picked / jnp.sum(picked, axis=-1, keepdims=True)

    gates, gate_back = jax.vjp(gate_values, logits)
    repeated = jnp.repeat(stream, 2, axis=0)
    outgoing = jnp.dot(dispatch_table, repeated, preferred_element_type=jnp.float32).astype(
        jnp.bfloat16
    )
    outgoing = outgoing.reshape(experts, capacity, width)
    weight_rows_in, weight_rows_out = (
        lax.all_gather(expert_in[0], "blk", axis=0, tiled=True),
        lax.all_gather(expert_out[0], "blk", axis=0, tiled=True),
    )
    arrived = lax.all_to_all(outgoing, "exp", split_axis=0, concat_axis=0, tiled=True)
    pre_act = jnp.einsum("scd,hd->sch", arrived, weight_rows_in, preferred_element_type=jnp.float32)
    expert_hidden = gelu_tanh(pre_act).astype(jnp.bfloat16)
    result = jnp.einsum(
        "sch,hd->scd", expert_hidden, weight_rows_out, preferred_element_type=jnp.float32
    ).astype(jnp.bfloat16)
    received, pre_act, returned = (arrived, pre_act, to_sources(result))
    expert_rows = jnp.einsum(
        "ps,pd->sd",
        dispatch_table,
        returned.reshape(experts * capacity, width),
        preferred_element_type=jnp.float32,
    )
    expert_rows = expert_rows.reshape(own_rows, 2, width)
    mixture = gates[:, 0:1] * expert_rows[:, 0] + gates[:, 1:2] * expert_rows[:, 1]
    stream_two = stream.astype(jnp.float32) + mixture
    normed, norm_back = jax.vjp(rms_gain, stream_two, gain_second)
    layer_out = normed.astype(jnp.bfloat16)
    grad_two, gain_part = norm_back(cotangent.astype(jnp.float32))
    gate_grads = jnp.sum(expert_rows * grad_two[:, None, :], axis=-1)
    assigned_grads = (
        (gates[..., None] * grad_two[:, None, :]).astype(jnp.bfloat16).reshape(2 * own_rows, width)
    )
    grad_outgoing = jnp.dot(
        dispatch_table, assigned_grads, preferred_element_type=jnp.float32
    ).astype(jnp.bfloat16)
    grad_arrived = lax.all_to_all(
        grad_outgoing.reshape(experts, capacity, width),
        "exp",
        split_axis=0,
        concat_axis=0,
        tiled=True,
    )
    again_in, again_out = (
        lax.all_gather(expert_in[0], "blk", axis=0, tiled=True),
        lax.all_gather(expert_out[0], "blk", axis=0, tiled=True),
    )
    hidden_full, gelu_back = jax.vjp(gelu_tanh, pre_act)
    hidden = hidden_full.astype(jnp.bfloat16)
    hidden_grad = jnp.einsum(
        "scd,hd->sch", grad_arrived, again_out, preferred_element_type=jnp.float32
    )
    pre_grad = gelu_back(hidden_grad)[0].astype(jnp.bfloat16)
    term_in = jnp.einsum("sch,scd->hd", pre_grad, received, preferred_element_type=jnp.float32)
    term_out = jnp.einsum("sch,scd->hd", hidden, grad_arrived, preferred_element_type=jnp.float32)
    summed_grads = lax.psum_scatter(
        (jnp.concatenate([term_in, term_out], axis=1) * grad_scale).astype(jnp.bfloat16),
        "blk",
        scatter_dimension=0,
        tiled=True,
    ).astype(jnp.float32)
    expert_in_grad = summed_grads[None, :, :width]
    expert_out_grad = summed_grads[None, :, width:]
    rows_back = jnp.einsum(
        "sch,hd->scd", pre_grad, again_in, preferred_element_type=jnp.float32
    ).astype(jnp.bfloat16)
    back_home = to_sources(rows_back)
    back_rows = jnp.einsum(
        "ps,pd->sd",
        dispatch_table,
        back_home.reshape(experts * capacity, width),
        preferred_element_type=jnp.float32,
    )
    back_rows = back_rows.reshape(own_rows, 2, width)
    logit_grad = gate_back(gate_grads)[0]
    router_part = (
        jnp.dot(logit_grad.T, stream.astype(jnp.float32), precision=lax.Precision.HIGHEST)
        * grad_scale
    )
    router_grad, gain_grad = lax.psum((router_part, gain_part * grad_scale), ("blk", "exp"))
    router_term = jnp.dot(
        logit_grad, router_weight.astype(jnp.float32), precision=lax.Precision.HIGHEST
    )
    stream_grad = (grad_two + (back_rows[:, 0] + back_rows[:, 1]) + router_term).astype(
        jnp.bfloat16
    )
    return (layer_out, stream_grad, expert_in_grad, expert_out_grad, router_grad, gain_grad)


def solution(mesh):
    placed = (
        P("blk", None),
        P(None, "exp", None),
        P("exp", None),
        P(),
        P(),
        P(),
        P("exp", "blk", None),
        P("exp", "blk", None),
        P(("blk", "exp"), None),
        P(("blk", "exp"), None),
    )
    return jax.shard_map(
        local,
        mesh=mesh,
        in_specs=placed,
        out_specs=(
            P(("blk", "exp"), None),
            P(("blk", "exp"), None),
            P("exp", "blk", None),
            P("exp", "blk", None),
            P(),
            P(),
        ),
        check_vma=False,
    )
```

profile of v0, /device:TPU:1, one launch (start us, length us, event | category | flops | bytes accessed | tf_op | source)
XLA Modules:
  0.0 604.8 jit_solution(10231152198393182954)
XLA Ops:
  7.2 2.7 convolution_convert_fusion.1
  12.3 37.7 %all-gather.6.cloned.1.call-done = bf16[2,32,24576]{2,1,0:T(8,128)(2,1)} async-done(((bf16[2,32,1536]{2,1,0:T(8,128)(2,1)}), bf16[2,32,24576]{2,1,0:T(8,128)(2,1)}) %all-gather.6.cloned.1.call-update) | async-done | bytes 3145744 | tf_op jit(solution)/shard_map/all_gather | solution.py:60
  50.0 3.7 copy.60
  53.7 3.4 copy.66
  57.1 231.9 %while.15 = (s32[]{:T(128)}, f32[1,1536]{1,0:T(1,128)S(1)}, f32[1,1536]{1,0:T(1,128)S(1)}, f32[1,1536,32]{1,2,0:T(8,128)S(1)}, bf16[24,2,1,32,1024]{4,3,2,1,0:T(...) while((s32[]{:T(128)}, f32[1,1536]{1,0:T(1,128)S(1)}, ...), condition=%wide.region_3.4_spmd.clone, body=%wide.region_0.3_spmd.clone.sunk | while | flops 214066176 | bytes 44767396 | solution.py:88
  59.1 2.6 copy-done.1
  62.8 4.0 fusion.103
  72.5 4.0 fusion.103
  78.4 2.6 copy-done.1
  82.1 4.0 fusion.103
  88.1 2.6 copy-done.1
  91.8 4.0 fusion.103
  101.5 4.0 fusion.103
  111.1 4.0 fusion.103
  120.8 4.0 fusion.103
  130.5 4.0 fusion.103
  140.1 4.0 fusion.103
  149.8 4.0 fusion.103
  159.4 4.0 fusion.103
  169.1 4.0 fusion.103
  178.8 4.0 fusion.103
  188.4 4.0 fusion.103
  198.1 4.0 fusion.103
  207.8 4.0 fusion.103
  217.4 4.0 fusion.103
  227.1 4.0 fusion.103
  236.7 4.0 fusion.103
  246.4 4.0 fusion.103
  256.1 4.0 fusion.103
  265.7 4.0 fusion.103
  275.4 4.0 fusion.103
  285.1 4.0 fusion.103
  293.9 69.8 %reduce-scatter.5.cloned.1.call-done = bf16[192,512]{1,0:T(8,128)(2,1)} async-done(((bf16[1536,512]{1,0:T(8,128)(2,1)}), bf16[192,512]{1,0:T(8,128)(2,1)}) %reduce-scatter.5.cloned.1.call-update) | async-done | bytes 196624 | tf_op jit(solution)/shard_map/reduce_scatter | solution.py:92
  367.9 3.7 all-to-all-start
  373.0 32.2 %all-gather.8.cloned.1.call-done = bf16[1,2048,512]{2,1,0:T(8,128)(2,1)} async-done(((bf16[1,128,512]{2,1,0:T(8,128)(2,1)}), bf16[1,2048,512]{2,1,0:T(8,128)(2,1)}) %all-gather.8.cloned.1.call-update) | async-done | bytes 2097168 | tf_op jit(solution)/shard_map/all_gather | solution.py:126
  405.2 6.1 %fusion.32 = f32[8,96,2048]{2,1,0:T(8,128)} fusion(bf16[8,96,512]{2,1,0:T(8,128)(2,1)S(1)} %all-to-all-done, bf16[1,2048,512]{2,1,0:T(8,128)(2,1)} %all-gather.8.cloned.1.call-done), kind=kOutput, calls=%fused_computation.46 | convolution fusion | flops 1610612736 | bytes 9175040 | tf_op jit(solution)/shard_map/scd,hd->sch/dot_general | solution.py:130
  411.2 30.7 %all-gather.10.cloned.1.call-done = bf16[1,2048,512]{2,1,0:T(8,128)(2,1)} async-done(((bf16[1,128,512]{2,1,0:T(8,128)(2,1)}), bf16[1,2048,512]{2,1,0:T(8,128)(2,1)}) %all-gather.10.cloned.1.call-update) | async-done | bytes 2097168 | tf_op jit(solution)/shard_map/all_gather | solution.py:127
  441.9 6.5 %fusion.38 = bf16[8,96,512]{2,1,0:T(8,128)(2,1)} fusion(bf16[1,2048,512]{2,1,0:T(8,128)(2,1)} %all-gather.10.cloned.1.call-done, f32[8,96,2048]{2,1,0:T(8,128)} %fusion.32), kind=kOutput, calls=%fused_computation.50 | convolution fusion | flops 1625161728 | bytes 9175040 | tf_op jit(solution)/shard_map/sch,hd->scd/dot_general | solution.py:132
  448.4 5.9 all-to-all-start.1
  454.9 14.0 %all-to-all-done.1 = bf16[8,96,512]{2,1,0:T(8,128)(2,1)S(1)} async-done(((bf16[8,96,512]{2,1,0:T(8,128)(2,1)}), bf16[8,96,512]{2,1,0:T(8,128)(2,1)S(1)}, u32[]{:S(2)}, u32[]{:S(2)}) %all-to-all-start.1) | async-done | bytes 786464 | tf_op jit(solution)/shard_map/all_to_all | solution.py:21
  475.3 16.2 %all_to_all.20 = bf16[8,96,512]{2,1,0:T(8,128)(2,1)S(1)} all-to-all(bf16[8,96,512]{2,1,0:T(8,128)(2,1)S(1)} %bitcast.131), channel_id=1, replica_groups=mesh['blk'=16,'exp'=8] {'exp'}, dimensions={0} | all-to-all | bytes 1572864 | tf_op jit(solution)/shard_map/all_to_all | solution.py:155
  491.5 7.8 %fusion.25 = bf16[8,96,2048]{2,1,0:T(8,128)(2,1)S(1)} fusion(f32[8,96,2048]{2,1,0:T(8,128)} %fusion.32, bf16[8,96,512]{2,1,0:T(8,128)(2,1)S(1)} %all_to_all.20, bf16[1,2048,512]{2,1,0:T(8,128)(2,1)} %all-gather.10.cloned.1.call-done), kind=kOutput, calls=%fused_computation.32 | convolution fusion | flops 1642070016 | bytes 12320768 | tf_op jit(solution)/shard_map/scd,hd->sch/dot_general | solution.py:168
  499.3 2.9 convolution_bitcast_fusion
  504.1 2.6 fusion.18
  506.7 6.4 %copy.56 = bf16[2048,1024]{1,0:T(8,128)(2,1)} copy(bf16[2048,1024]{0,1:T(8,128)(2,1)} %fusion.18) | data formatting | bytes 8388608
  513.3 5.3 fusion.35
  518.6 3.5 all-to-all-start.3
  522.4 71.4 %all-reduce = (f32[8,512]{1,0:T(8,128)}, f32[512]{0:T(512)}) all-reduce(f32[8,512]{1,0:T(8,128)S(1)} %convolution_multiply_fusion, f32[512]{0:T(512)S(1)} %broadcast_multiply_fusion), channel_id=1, replica_groups=mesh['blk'=16,'exp'=8] {'blk','exp'}, use_global_device_ids=true, to_apply=%region_17.18 | all-reduce | flops 4608 | bytes 36864 | tf_op jit(solution)/shard_map/psum | solution.py:198
  (254 shorter events, 153.6 us)
Async XLA Ops:
  7.2 281.9 %copy-start = (bf16[32,512]{1,0:T(8,128)(2,1)S(1)}, bf16[32,512]{1,0:T(8,128)(2,1)}, u32[]{:S(2)}) copy-start(bf16[32,512]{1,0:T(8,128)(2,1)} %param.14) | copy-start | bytes 98308
  7.2 42.8 %all-gather.6.cloned.1.call-start = ((), (), s32[]{:S(2)}) async-start(), calls=%async_computation.6 | async-start | bytes 3342336 | tf_op jit(solution)/shard_map/all_gather | solution.py:60
  10.0 353.7 %reduce-scatter.5.cloned.1.call-start = ((), (), s32[]{:S(2)}) async-start(), calls=%async_computation.7 | async-start | bytes 1769472 | tf_op jit(solution)/shard_map/reduce_scatter | solution.py:92
  57.1 235.2 %copy-start.5 = (s32[192,2]{0,1:T(2,128)S(1)}, s32[192,2]{0,1:T(2,128)}, u32[]{:S(2)}) copy-start(s32[192,2]{0,1:T(2,128)} %param.20) | copy-start | bytes 4612
  57.1 307.8 %copy-start.7 = (f32[512]{0:T(512)S(1)}, f32[512]{0:T(512)}, u32[]{:S(2)}) copy-start(f32[512]{0:T(512)} %param.16) | copy-start | bytes 6148
  59.0 2.7 copy-start.1
  68.7 2.7 copy-start.1
  78.4 2.7 copy-start.1
  88.0 2.7 copy-start.1
  97.7 2.7 copy-start.1
  107.4 2.7 copy-start.1
  117.0 2.7 copy-start.1
  126.7 2.7 copy-start.1
  136.3 2.7 copy-start.1
  146.0 2.7 copy-start.1
  155.7 2.7 copy-start.1
  165.3 2.7 copy-start.1
  175.0 2.7 copy-start.1
  184.7 2.7 copy-start.1
  194.3 2.7 copy-start.1
  204.0 2.7 copy-start.1
  213.7 2.7 copy-start.1
  223.3 2.7 copy-start.1
  233.0 2.7 copy-start.1
  242.6 2.7 copy-start.1
  252.3 2.7 copy-start.1
  262.0 2.7 copy-start.1
  271.6 2.7 copy-start.1
  281.3 2.7 copy-start.1
  291.0 114.2 %all-gather.8.cloned.1.call-start = ((), (), s32[]{:S(2)}) async-start(), calls=%async_computation.8 | async-start | bytes 2228224 | tf_op jit(solution)/shard_map/all_gather | solution.py:126
  291.7 150.2 %all-gather.10.cloned.1.call-start = ((), (), s32[]{:S(2)}) async-start(), calls=%async_computation.9 | async-start | bytes 2228224 | tf_op jit(solution)/shard_map/all_gather | solution.py:127
  367.9 37.2 %all-to-all-start = ((bf16[8,96,512]{2,1,0:T(8,128)(2,1)}), bf16[8,96,512]{2,1,0:T(8,128)(2,1)S(1)}, u32[]{:S(2)}, u32[]{:S(2)}) async-start(bf16[8,96,512]{2,1,0:T(8,128)(2,1)} %bitcast.8), calls=%async_computation.1 | async-start | bytes 1572864 | tf_op jit(solution)/shard_map/all_to_all | solution.py:129
  411.2 43.1 %copy-start.4 = (bf16[8,512]{1,0:T(8,128)(2,1)S(1)}, bf16[8,512]{1,0:T(8,128)(2,1)}, u32[]{:S(2)}) copy-start(bf16[8,512]{1,0:T(8,128)(2,1)} %param.15) | copy-start | bytes 24580
  411.2 59.4 %copy-start.2 = (bf16[192,512]{1,0:T(8,128)(2,1)S(1)}, bf16[192,512]{1,0:T(8,128)(2,1)}, u32[]{:S(2)}) copy-start(bf16[192,512]{1,0:T(8,128)(2,1)} %param.21) | copy-start | bytes 589828
  411.2 59.4 %copy-start.6 = (f32[512]{0:T(512)S(1)}, f32[512]{0:T(512)}, u32[]{:S(2)}) copy-start(f32[512]{0:T(512)} %param.17) | copy-start | bytes 6148
  448.4 20.5 %all-to-all-start.1 = ((bf16[8,96,512]{2,1,0:T(8,128)(2,1)}), bf16[8,96,512]{2,1,0:T(8,128)(2,1)S(1)}, u32[]{:S(2)}, u32[]{:S(2)}) async-start(bf16[8,96,512]{2,1,0:T(8,128)(2,1)} %fusion.38), calls=%async_computation.2 | async-start | bytes 1572864 | tf_op jit(solution)/shard_map/all_to_all | solution.py:21
  454.3 141.1 %reduce-scatter.7.cloned.1.call-start = ((), (), s32[]{:S(2)}) async-start(), calls=%async_computation.10 | async-start | bytes 4456448
  475.3 24.0 %slice-start = ((s8[6291456]{0:T(1024)(128)(4,1)}), s8[4194304]{0:T(1024)(128)(4,1)S(1)}, s32[]{:S(2)}) async-start(s8[6291456]{0:T(1024)(128)(4,1)} %bitcast.127), calls=%async_computation.11 | async-start | bytes 8388608
  491.5 7.8 %slice-start.1 = ((s8[6291456]{0:T(1024)(128)(4,1)}), s8[2097152]{0:T(1024)(128)(4,1)S(1)}, s32[]{:S(2)}) async-start(s8[6291456]{0:T(1024)(128)(4,1)} %bitcast.127), calls=%async_computation.12 | async-start | bytes 4194304
  499.3 2.9 copy-start.8
  513.3 80.5 %copy-start.3 = (pred[192,2,768]{2,1,0:T(4,128)(4,1)S(1)}, pred[192,2,768]{2,1,0:T(4,128)(4,1)}, u32[]{:S(2)}) copy-start(pred[192,2,768]{2,1,0:T(4,128)(4,1)} %eq.74) | copy-start | bytes 884740
  518.6 75.2 %all-to-all-start.3 = ((bf16[8,96,512]{2,1,0:T(8,128)(2,1)}), bf16[8,96,512]{2,1,0:T(8,128)(2,1)S(1)}, u32[]{:S(2)}, u32[]{:S(2)}) async-start(bf16[8,96,512]{2,1,0:T(8,128)(2,1)} %fusion.35), calls=%async_computation.4 | async-start | bytes 1572864 | tf_op jit(solution)/shard_map/all_to_all | solution.py:21
Sparse Core Ops, SparseCore 0:
  10.2 39.6 all-gather.5
  291.1 72.5 reduce-scatter.4
  365.4 39.6 all-gather.7
  406.7 35.1 all-gather.9
  513.2 72.5 reduce-scatter.6
where the time goes:
time: 607 us; the launch traced here: 605 us
  waiting for transfers between devices  186 us (31%)
  matrix products  183 us (30%)
  blocking collectives  87.7 us (14%)
  local copies, waits for them, and re-layouts  84.3 us (14%)
  other arithmetic  35.3 us (6%)
  between operations  14.2 us (2%)
  starting transfers between devices  13.4 us (2%)
    dot_general x24, matrix products, key_step(): jnp.einsum('htk,hfk->htf', weights.astype(jnp.bfloat16), key_block[1], pr...  95.5 us
    psum x1, blocking collectives, local(): lax.psum((router_part, gain_part * grad_scale), ('blk', 'exp'))  71.4 us
    reduce_scatter x1, waiting for transfers between devices, local(): lax.psum_scatter(jnp.dot(by_rows, output_weight, preferred_element_type=j...  69.8 us
    while x72, local copies, waits for them, and re-layouts  62.5 us
    dot_general x24, matrix products, key_step(): jnp.einsum('htf,hfk->htk', query_heads, key_block[0], preferred_element_t...  45.2 us
    all_gather x1, waiting for transfers between devices, local(): shard_piece = lax.all_gather(keys_values, 'blk', axis=2, tiled=True)  37.7 us
    all_gather x1, waiting for transfers between devices, local(): lax.all_gather(expert_in[0], 'blk', axis=0, tiled=True)  32.2 us
    all_gather x1, waiting for transfers between devices, local(): lax.all_gather(expert_out[0], 'blk', axis=0, tiled=True)  30.7 us
  transfers between devices with their start and end apart: 8, of which 5 were waited for; matrix products, arithmetic and copies ran while one was open for 4% of the time, Pallas kernels for 0%

commit v1 on v0

--- a/solution.py
+++ b/solution.py
@@ -195,7 +195,9 @@
         jnp.dot(logit_grad.T, stream.astype(jnp.float32), precision=lax.Precision.HIGHEST)
         * grad_scale
     )
-    router_grad, gain_grad = lax.psum((router_part, gain_part * grad_scale), ("blk", "exp"))
+    router_grad, gain_grad = lax.psum(
+        lax.psum((router_part, gain_part * grad_scale), axis_name="exp"), axis_name="blk"
+    )
     router_term = jnp.dot(
         logit_grad, router_weight.astype(jnp.float32), precision=lax.Precision.HIGHEST
     )

time: 607 us -> 632 us (1.041)
  blocking collectives: 87.7 us -> 110 us
    psum x1 -> x2, blocking collectives: 71.4 us -> 93.7 us  [the longest x1 56.7 us: local(): lax.psum(lax.psum((router_part, gain_part * grad_scale), axis_name='exp')...]
where the time goes in v1:
time: 632 us; the launch traced here: 627 us
  waiting for transfers between devices  186 us (29%)
  matrix products  183 us (29%)
  blocking collectives  110 us (17%)
  local copies, waits for them, and re-layouts  84.3 us (13%)
  other arithmetic  35.3 us (6%)
  between operations  14.2 us (2%)
  starting transfers between devices  13.4 us (2%)
    dot_general x24, matrix products, key_step(): jnp.einsum('htk,hfk->htf', weights.astype(jnp.bfloat16), key_block[1], pr...  95.5 us
    reduce_scatter x1, waiting for transfers between devices, local(): lax.psum_scatter(jnp.dot(by_rows, output_weight, preferred_element_type=j...  69.8 us
    while x72, local copies, waits for them, and re-layouts  62.5 us
    psum x1, blocking collectives, local(): lax.psum(lax.psum((router_part, gain_part * grad_scale), axis_name='exp')...  56.7 us
    dot_general x24, matrix products, key_step(): jnp.einsum('htf,hfk->htk', query_heads, key_block[0], preferred_element_t...  45.2 us
    all_gather x1, waiting for transfers between devices, local(): shard_piece = lax.all_gather(keys_values, 'blk', axis=2, tiled=True)  37.7 us
    psum x1, blocking collectives, local(): lax.psum((router_part, gain_part * grad_scale), axis_name='exp')  37 us
    all_gather x1, waiting for transfers between devices, local(): lax.all_gather(expert_in[0], 'blk', axis=0, tiled=True)  32.2 us
  transfers between devices with their start and end apart: 8, of which 5 were waited for; matrix products, arithmetic and copies ran while one was open for 4% of the time, Pallas kernels for 0%

profile of v1, /device:TPU:1, one launch (start us, length us, event | category | flops | bytes accessed | tf_op | source)
XLA Modules:
  0.0 627.0 jit_solution(125966703579476056)
XLA Ops:
  7.2 2.7 convolution_convert_fusion.1
  12.3 37.7 %all-gather.6.cloned.1.call-done = bf16[2,32,24576]{2,1,0:T(8,128)(2,1)} async-done(((bf16[2,32,1536]{2,1,0:T(8,128)(2,1)}), bf16[2,32,24576]{2,1,0:T(8,128)(2,1)}) %all-gather.6.cloned.1.call-update) | async-done | bytes 3145744 | tf_op jit(solution)/shard_map/all_gather | solution.py:60
  50.0 3.7 copy.60
  53.7 3.4 copy.66
  57.1 231.9 %while.15 = (s32[]{:T(128)}, f32[1,1536]{1,0:T(1,128)S(1)}, f32[1,1536]{1,0:T(1,128)S(1)}, f32[1,1536,32]{1,2,0:T(8,128)S(1)}, bf16[24,2,1,32,1024]{4,3,2,1,0:T(...) while((s32[]{:T(128)}, f32[1,1536]{1,0:T(1,128)S(1)}, ...), condition=%wide.region_3.4_spmd.clone, body=%wide.region_0.3_spmd.clone.sunk | while | flops 214066176 | bytes 44767396 | solution.py:88
  59.1 2.6 copy-done.1
  62.8 4.0 fusion.103
  72.5 4.0 fusion.103
  78.4 2.6 copy-done.1
  82.1 4.0 fusion.103
  91.8 4.0 fusion.103
  101.5 4.0 fusion.103
  111.1 4.0 fusion.103
  120.8 4.0 fusion.103
  130.5 4.0 fusion.103
  140.1 4.0 fusion.103
  149.8 4.0 fusion.103
  159.4 4.0 fusion.103
  169.1 4.0 fusion.103
  178.8 4.0 fusion.103
  188.4 4.0 fusion.103
  198.1 4.0 fusion.103
  207.8 4.0 fusion.103
  217.4 4.0 fusion.103
  227.1 4.0 fusion.103
  236.7 4.0 fusion.103
  246.4 4.0 fusion.103
  256.1 4.0 fusion.103
  265.7 4.0 fusion.103
  275.4 4.0 fusion.103
  285.1 4.0 fusion.103
  293.9 69.8 %reduce-scatter.5.cloned.1.call-done = bf16[192,512]{1,0:T(8,128)(2,1)} async-done(((bf16[1536,512]{1,0:T(8,128)(2,1)}), bf16[192,512]{1,0:T(8,128)(2,1)}) %reduce-scatter.5.cloned.1.call-update) | async-done | bytes 196624 | tf_op jit(solution)/shard_map/reduce_scatter | solution.py:92
  367.9 3.7 all-to-all-start
  373.0 32.2 %all-gather.8.cloned.1.call-done = bf16[1,2048,512]{2,1,0:T(8,128)(2,1)} async-done(((bf16[1,128,512]{2,1,0:T(8,128)(2,1)}), bf16[1,2048,512]{2,1,0:T(8,128)(2,1)}) %all-gather.8.cloned.1.call-update) | async-done | bytes 2097168 | tf_op jit(solution)/shard_map/all_gather | solution.py:126
  405.2 6.1 fusion.32
  411.2 30.7 %all-gather.10.cloned.1.call-done = bf16[1,2048,512]{2,1,0:T(8,128)(2,1)} async-done(((bf16[1,128,512]{2,1,0:T(8,128)(2,1)}), bf16[1,2048,512]{2,1,0:T(8,128)(2,1)}) %all-gather.10.cloned.1.call-update) | async-done | bytes 2097168 | tf_op jit(solution)/shard_map/all_gather | solution.py:127
  441.9 6.5 %fusion.38 = bf16[8,96,512]{2,1,0:T(8,128)(2,1)} fusion(bf16[1,2048,512]{2,1,0:T(8,128)(2,1)} %all-gather.10.cloned.1.call-done, f32[8,96,2048]{2,1,0:T(8,128)} %fusion.32), kind=kOutput, calls=%fused_computation.50 | convolution fusion | flops 1625161728 | bytes 9175040 | tf_op jit(solution)/shard_map/sch,hd->scd/dot_general | solution.py:132
  448.4 5.9 all-to-all-start.1
  454.9 14.0 %all-to-all-done.1 = bf16[8,96,512]{2,1,0:T(8,128)(2,1)S(1)} async-done(((bf16[8,96,512]{2,1,0:T(8,128)(2,1)}), bf16[8,96,512]{2,1,0:T(8,128)(2,1)S(1)}, u32[]{:S(2)}, u32[]{:S(2)}) %all-to-all-start.1) | async-done | bytes 786464 | tf_op jit(solution)/shard_map/all_to_all | solution.py:21
  475.3 16.2 %all_to_all.20 = bf16[8,96,512]{2,1,0:T(8,128)(2,1)S(1)} all-to-all(bf16[8,96,512]{2,1,0:T(8,128)(2,1)S(1)} %bitcast.131), channel_id=1, replica_groups=mesh['blk'=16,'exp'=8] {'exp'}, dimensions={0} | all-to-all | bytes 1572864 | tf_op jit(solution)/shard_map/all_to_all | solution.py:155
  491.5 7.8 %fusion.25 = bf16[8,96,2048]{2,1,0:T(8,128)(2,1)S(1)} fusion(f32[8,96,2048]{2,1,0:T(8,128)} %fusion.32, bf16[8,96,512]{2,1,0:T(8,128)(2,1)S(1)} %all_to_all.20, bf16[1,2048,512]{2,1,0:T(8,128)(2,1)} %all-gather.10.cloned.1.call-done), kind=kOutput, calls=%fused_computation.32 | convolution fusion | flops 1642070016 | bytes 12320768 | tf_op jit(solution)/shard_map/scd,hd->sch/dot_general | solution.py:168
  499.3 2.9 convolution_bitcast_fusion
  504.1 2.6 fusion.18
  506.7 6.4 %copy.56 = bf16[2048,1024]{1,0:T(8,128)(2,1)} copy(bf16[2048,1024]{0,1:T(8,128)(2,1)} %fusion.18) | data formatting | bytes 8388608
  513.3 5.3 fusion.35
  518.6 3.5 all-to-all-start.3
  522.4 37.0 %all-reduce.1 = (f32[8,512]{1,0:T(8,128)S(1)}, f32[512]{0:T(512)S(1)}) all-reduce(f32[8,512]{1,0:T(8,128)S(1)} %convolution_multiply_fusion, f32[512]{0:T(512)S(1)} %broadcast_multiply_fusion), channel_id=1, replica_groups=mesh['blk'=16,'exp'=8] {'exp'}, use_global_device_ids=true, to_apply=%region_17.18 | all-reduce | flops 4608 | bytes 36864 | tf_op jit(solution)/shard_map/psum | solution.py:199
  559.4 56.7 %all-reduce = (f32[8,512]{1,0:T(8,128)}, f32[512]{0:T(512)}) all-reduce(f32[8,512]{1,0:T(8,128)S(1)} %get-tuple-element.130, f32[512]{0:T(512)S(1)} %get-tuple-element.131), channel_id=1, replica_groups=mesh['blk'=16,'exp'=8] {'blk'}, use_global_device_ids=true, to_apply=%region_18.19 | all-reduce | flops 4608 | bytes 36864 | tf_op jit(solution)/shard_map/psum | solution.py:198
  (255 shorter events, 156.2 us)
Async XLA Ops:
  7.2 281.9 %copy-start = (bf16[32,512]{1,0:T(8,128)(2,1)S(1)}, bf16[32,512]{1,0:T(8,128)(2,1)}, u32[]{:S(2)}) copy-start(bf16[32,512]{1,0:T(8,128)(2,1)} %param.14) | copy-start | bytes 98308
  7.2 42.8 %all-gather.6.cloned.1.call-start = ((), (), s32[]{:S(2)}) async-start(), calls=%async_computation.6 | async-start | bytes 3342336 | tf_op jit(solution)/shard_map/all_gather | solution.py:60
  10.0 353.7 %reduce-scatter.5.cloned.1.call-start = ((), (), s32[]{:S(2)}) async-start(), calls=%async_computation.7 | async-start | bytes 1769472 | tf_op jit(solution)/shard_map/reduce_scatter | solution.py:92
  57.1 235.2 %copy-start.5 = (s32[192,2]{0,1:T(2,128)S(1)}, s32[192,2]{0,1:T(2,128)}, u32[]{:S(2)}) copy-start(s32[192,2]{0,1:T(2,128)} %param.20) | copy-start | bytes 4612
  57.1 307.8 %copy-start.7 = (f32[512]{0:T(512)S(1)}, f32[512]{0:T(512)}, u32[]{:S(2)}) copy-start(f32[512]{0:T(512)} %param.16) | copy-start | bytes 6148
  59.0 2.7 copy-start.1
  68.7 2.7 copy-start.1
  78.4 2.7 copy-start.1
  88.0 2.7 copy-start.1
  97.7 2.7 copy-start.1
  107.4 2.7 copy-start.1
  117.0 2.7 copy-start.1
  126.7 2.7 copy-start.1
  136.3 2.7 copy-start.1
  146.0 2.7 copy-start.1
  155.7 2.7 copy-start.1
  165.3 2.7 copy-start.1
  175.0 2.7 copy-start.1
  184.7 2.7 copy-start.1
  194.3 2.7 copy-start.1
  204.0 2.7 copy-start.1
  213.7 2.7 copy-start.1
  223.3 2.7 copy-start.1
  233.0 2.7 copy-start.1
  242.6 2.7 copy-start.1
  252.3 2.7 copy-start.1
  262.0 2.7 copy-start.1
  271.6 2.7 copy-start.1
  281.3 2.7 copy-start.1
  291.0 114.2 %all-gather.8.cloned.1.call-start = ((), (), s32[]{:S(2)}) async-start(), calls=%async_computation.8 | async-start | bytes 2228224 | tf_op jit(solution)/shard_map/all_gather | solution.py:126
  291.7 150.2 %all-gather.10.cloned.1.call-start = ((), (), s32[]{:S(2)}) async-start(), calls=%async_computation.9 | async-start | bytes 2228224 | tf_op jit(solution)/shard_map/all_gather | solution.py:127
  367.9 37.2 %all-to-all-start = ((bf16[8,96,512]{2,1,0:T(8,128)(2,1)}), bf16[8,96,512]{2,1,0:T(8,128)(2,1)S(1)}, u32[]{:S(2)}, u32[]{:S(2)}) async-start(bf16[8,96,512]{2,1,0:T(8,128)(2,1)} %bitcast.8), calls=%async_computation.1 | async-start | bytes 1572864 | tf_op jit(solution)/shard_map/all_to_all | solution.py:129
  411.2 43.1 %copy-start.4 = (bf16[8,512]{1,0:T(8,128)(2,1)S(1)}, bf16[8,512]{1,0:T(8,128)(2,1)}, u32[]{:S(2)}) copy-start(bf16[8,512]{1,0:T(8,128)(2,1)} %param.15) | copy-start | bytes 24580
  411.2 59.4 %copy-start.2 = (bf16[192,512]{1,0:T(8,128)(2,1)S(1)}, bf16[192,512]{1,0:T(8,128)(2,1)}, u32[]{:S(2)}) copy-start(bf16[192,512]{1,0:T(8,128)(2,1)} %param.21) | copy-start | bytes 589828
  411.2 59.4 %copy-start.6 = (f32[512]{0:T(512)S(1)}, f32[512]{0:T(512)}, u32[]{:S(2)}) copy-start(f32[512]{0:T(512)} %param.17) | copy-start | bytes 6148
  448.4 20.5 %all-to-all-start.1 = ((bf16[8,96,512]{2,1,0:T(8,128)(2,1)}), bf16[8,96,512]{2,1,0:T(8,128)(2,1)S(1)}, u32[]{:S(2)}, u32[]{:S(2)}) async-start(bf16[8,96,512]{2,1,0:T(8,128)(2,1)} %fusion.38), calls=%async_computation.2 | async-start | bytes 1572864 | tf_op jit(solution)/shard_map/all_to_all | solution.py:21
  454.3 163.3 %reduce-scatter.7.cloned.1.call-start = ((), (), s32[]{:S(2)}) async-start(), calls=%async_computation.10 | async-start | bytes 4456448
  475.3 24.0 %slice-start = ((s8[6291456]{0:T(1024)(128)(4,1)}), s8[4194304]{0:T(1024)(128)(4,1)S(1)}, s32[]{:S(2)}) async-start(s8[6291456]{0:T(1024)(128)(4,1)} %bitcast.127), calls=%async_computation.11 | async-start | bytes 8388608
  491.5 7.8 %slice-start.1 = ((s8[6291456]{0:T(1024)(128)(4,1)}), s8[2097152]{0:T(1024)(128)(4,1)S(1)}, s32[]{:S(2)}) async-start(s8[6291456]{0:T(1024)(128)(4,1)} %bitcast.127), calls=%async_computation.12 | async-start | bytes 4194304
  499.3 2.9 copy-start.8
  513.3 102.7 %copy-start.3 = (pred[192,2,768]{2,1,0:T(4,128)(4,1)S(1)}, pred[192,2,768]{2,1,0:T(4,128)(4,1)}, u32[]{:S(2)}) copy-start(pred[192,2,768]{2,1,0:T(4,128)(4,1)} %eq.74) | copy-start | bytes 884740
  518.6 97.5 %all-to-all-start.3 = ((bf16[8,96,512]{2,1,0:T(8,128)(2,1)}), bf16[8,96,512]{2,1,0:T(8,128)(2,1)S(1)}, u32[]{:S(2)}, u32[]{:S(2)}) async-start(bf16[8,96,512]{2,1,0:T(8,128)(2,1)} %fusion.35), calls=%async_computation.4 | async-start | bytes 1572864 | tf_op jit(solution)/shard_map/all_to_all | solution.py:21
Sparse Core Ops, SparseCore 0:
  10.2 39.6 all-gather.5
  291.1 72.5 reduce-scatter.4
  365.4 39.6 all-gather.7
  406.7 35.1 all-gather.9
  513.2 72.3 reduce-scatter.6
